TPU v7x, 256 devices: a whole 4x4x8 slice. The times are simulated.
256 devices in a mesh: pipe: 2 (over core), group: 16 (over x, y), local: 8 (over z).
Axes of the slice: x: 4, y: 4, z: 8, core: 2. Of those that a mesh axis runs over, the one named last changes fastest.
Arguments:
- output_grad: bfloat16 [2, 4096, 2048], P(None, ('group', 'local')), may hold values from -6 to 6
- carried_grad: bfloat16 [4096, 2048], P(('group', 'local')), may hold values from -6 to 6
- layer_inputs: bfloat16 [2, 2, 4096, 2048], P('pipe', None, ('group', 'local')), may hold values from -6 to 6
- expert_ids: int32 [2, 2, 4096, 6], P('pipe', None, ('group', 'local')), may hold values from 0 to 63, all different within a row; in each aligned block of 32 rows (0 to 31, 32 to 63, ..., all dimensions but the last counted through in order) at most 4 rows name the same one
- gate_prob: bfloat16 [2, 2, 4096, 6], P('pipe', None, ('group', 'local')), may hold values from 0.099609375 to 0.796875
- gate_weight: bfloat16 [2, 128, 2048, 704], P('pipe', ('group', 'local')), may hold values from -0.125 to 0.125
- up_weight: bfloat16 [2, 128, 2048, 704], P('pipe', ('group', 'local')), may hold values from -0.125 to 0.125
- down_weight: bfloat16 [2, 128, 704, 2048], P('pipe', ('group', 'local')), may hold values from -0.15625 to 0.15625
Outputs:
- input_grad: bfloat16 [2, 2, 4096, 2048], P('pipe', None, ('group', 'local'))
- gate_grad: bfloat16 [2, 2, 4096, 6], P('pipe', None, ('group', 'local'))
Inputs may be any that keep to these rules, and one draw needn't show every extreme that they name: `expert_ids`: each token names 6 different experts. Within each section and microbatch, the 32 tokens of one device (aligned blocks of rows) name any one expert at most 4 times.
All inputs are finite; a program needn't handle non-finite values.
Results may differ from a plain program's by a relative error of at most 0.0065.
Values may be sent and summed in bfloat16 or wider, within the bound.
A program may use at most 128 MiB of HBM per device.

v0:
```python
import functools

import jax
import jax.numpy as jnp
from jax import lax
from jax.experimental import pallas as pl
from jax.experimental.pallas import tpu as pltpu
from jax.sharding import PartitionSpec as P

MESH = pl.DeviceIdType.MESH
NX, NY, NZ = 4, 4, 8
NG = NX * NY
TOK, D, HALF, SLOTS = 32, 2048, 704, 4
ROWS = NG * TOK
ALL = NZ * TOK
HALVES = 2
W = D // HALVES
EXTRA = 128
WIDE = (W, W + EXTRA)
STEPS = ((4, 3), (3, 4))
NT = (((1,), (1,)), ((), ()))
F32, BF16 = jnp.float32, jnp.bfloat16


def nt_dot(a, b):
    return lax.dot_general(a, b, NT, preferred_element_type=F32)


def kernel(
    og_ref, cg_ref, xin_ref, ids_ref, pr_ref, wg_hbm, wu_hbm, wd_hbm,
    out_ref, gate_ref,
    wg, wu, wd, meta, own_grad, passed, finished,
    gathered, picked, arrived, sent_back, came_back0, came_back1, sent_wide,
    a_acc, b_acc, q_acc, da_buf, db_buf, dmat, cmat, mmat, p0, p1,
    rs_send, rs_recv,
    w_sem, meta_ss, meta_rs, ag_ss, ag_rs, x_ss, x_rs, r_ss, r_rs, rs_ss, rs_rs, pass_ss, pass_rs,
):
    pipe = lax.axis_index("pipe")
    g = lax.axis_index("group")
    z = lax.axis_index("local")
    x, y = g // NY, g % NY
    up = (pipe, g, lax.rem(z + 1, NZ))
    down = (pipe, g, lax.rem(z + NZ - 1, NZ))
    partner = (1 - pipe, g, z)
    came_back = (came_back0, came_back1)
    back_out = (sent_back, sent_wide)
    sums = (p0, p1)
    waits = []

    def remote(src, dst, ss, rs, device):
        copy = pltpu.make_async_remote_copy(
            src_ref=src, dst_ref=dst, send_sem=ss, recv_sem=rs, device_id=device, device_id_type=MESH
        )
        return copy

    loads = []
    for i, (h, v) in enumerate(((wg_hbm, wg), (wu_hbm, wu), (wd_hbm, wd))):
        copy = pltpu.make_async_copy(h, v, w_sem.at[i])
        copy.start()
        loads.append(copy)

    barrier = pltpu.get_barrier_semaphore()

    def plane_peer(i):
        diag, dx = i // NX, i % NX
        dy = lax.rem(diag - dx + NY, NY)
        return lax.rem(x + dx, NX) * NY + lax.rem(y + dy, NY)

    def greet(i, carry):
        pl.semaphore_signal(barrier, inc=1, device_id=(pipe, plane_peer(i), z), device_id_type=MESH)
        return carry

    for device in (up, down, partner):
        pl.semaphore_signal(barrier, inc=1, device_id=device, device_id_type=MESH)
    lax.fori_loop(1, NG, greet, 0)

    lane = lax.broadcasted_iota(jnp.int32, (TOK, EXTRA), 1)
    lower = (
        lax.broadcasted_iota(jnp.int32, (TOK, TOK), 0) > lax.broadcasted_iota(jnp.int32, (TOK, TOK), 1)
    ).astype(BF16)
    for m in range(2):
        ids = ids_ref[m]
        probs = pr_ref[m].astype(F32)
        chosen = jnp.zeros((TOK, EXTRA), F32)
        weight = jnp.zeros((TOK, EXTRA), F32)
        for k in range(ids.shape[1]):
            chosen += (lane == ids[:, k : k + 1]).astype(F32)
            weight += jnp.where(lane == ids[:, k : k + 1] + 64, probs[:, k : k + 1], 0.0)
        before = jnp.dot(lower, chosen.astype(BF16), preferred_element_type=F32)
        meta[z, m] = (chosen * (before + 1.0) + weight).astype(BF16)
    is_last = pipe == 1
    own_grad[0] = jnp.where(is_last, og_ref[0].astype(F32), cg_ref[...].astype(F32)).astype(BF16)

    pl.semaphore_wait(barrier, NG - 1 + 3)

    def ring_items(first_src, at, ss, rs, counts):
        nr, nl = counts

        def hop(direction, s):
            if direction == 0:
                origin = lax.rem(z - s + NZ, NZ)
                device, slot = up, s
            else:
                origin = lax.rem(z + s, NZ)
                device, slot = down, nr + s
            src = first_src if s == 0 else at(origin)
            return remote(src, at(origin), ss.at[slot], rs.at[slot], device)

        def step(s):
            for direction, count in ((0, nr), (1, nl)):
                if s >= 1 and s - 1 < count:
                    hop(direction, s - 1).wait_recv()
                if s < count:
                    copy = hop(direction, s)
                    copy.start()
                    waits.append(copy)

        return step, max(nr, nl) + 1

    def gather_item(kind, m, c):
        src = (xin_ref.at[m] if kind == 0 else own_grad.at[m]).at[:, pl.ds(c * W, W)]
        return ring_items(
            src, lambda o: gathered.at[kind, m, c, o], ag_ss.at[kind, m, c], ag_rs.at[kind, m, c], STEPS[c]
        )

    def place_own(kind, m):
        for c in range(HALVES):
            src = xin_ref[m] if kind == 0 else own_grad[m]
            gathered[kind, m, c, z] = src[:, c * W : (c + 1) * W]

    def run_items(items, lag=2):
        order = sorted((i + lag * s, i, s) for i, (_, n) in enumerate(items) for s in range(n))
        for _, i, s in order:
            items[i][0](s)
            if s == items[i][1] - 1 and len(items[i]) > 2:
                pass
            yield i, s == items[i][1] - 1

    def fan_out(buf, dst, ss, rs):
        def send(i, carry):
            peer = plane_peer(i)
            remote(buf.at[peer], dst.at[g], ss, rs, (pipe, peer, z)).start()
            return carry

        lax.fori_loop(1, NG, send, 0)
        dst[g] = buf[g]

    def drained(buf, sem):
        pltpu.make_async_copy(buf.at[pl.ds(0, NG - 1)], buf.at[pl.ds(0, NG - 1)], sem).wait()

    row_e = lax.broadcasted_iota(jnp.int32, (ROWS, EXTRA), 0) // TOK * 4 + z // 2
    row_lane = lax.broadcasted_iota(jnp.int32, (ROWS, EXTRA), 1)

    def build_maps():
        sel_slot = (row_lane == row_e).astype(BF16)
        sel_prob = (row_lane == row_e + 64).astype(BF16)
        r0 = lax.broadcasted_iota(jnp.int32, (ROWS, ALL), 0)
        t1 = lax.broadcasted_iota(jnp.int32, (ROWS, ALL), 1)
        want0 = jnp.where(r0 % TOK // SLOTS == t1 // TOK, r0 % SLOTS + 1, -1).astype(F32)
        r1 = lax.broadcasted_iota(jnp.int32, (ALL, ROWS), 1)
        t0 = lax.broadcasted_iota(jnp.int32, (ALL, ROWS), 0)
        want1 = jnp.where(r1 % TOK // SLOTS == t0 // TOK, r1 % SLOTS + 1, -1).astype(F32)
        for m in range(2):
            table = meta[:, m].reshape(ALL, EXTRA)
            dmat[m] = (nt_dot(sel_slot, table) == want0).astype(BF16)
            hit = nt_dot(table, sel_slot) == want1
            mmat[m] = hit.astype(BF16)
            cmat[m] = jnp.where(hit, nt_dot(table, sel_prob), 0.0).astype(BF16)

    def dispatch(kind, m, c):
        tokens = gathered[kind, m, c].reshape(ALL, W)
        half = ROWS // 2

        def pick(i, carry):
            rows = dmat[m, pl.ds(i * half, half), :]
            got = jnp.dot(rows, tokens, preferred_element_type=F32).astype(BF16)
            picked[kind, m, c, pl.ds(i * NG // 2, NG // 2)] = got.reshape(NG // 2, TOK, W)
            return carry

        lax.fori_loop(0, 2, pick, 0)
        fan_out(picked.at[kind, m, c], arrived.at[kind, m, c], x_ss.at[kind, m, c], x_rs.at[kind, m, c])

    def project(kind, m, c, pairs):
        drained(arrived.at[kind, m, c], x_rs.at[kind, m, c])
        blocks = NG // 2

        def part(i, carry):
            rows = arrived[kind, m, c, pl.ds(i * blocks, blocks)].reshape(blocks * TOK, W)
            at = pl.ds(pl.multiple_of(i * blocks * TOK, blocks * TOK), blocks * TOK)
            for weight, acc in pairs:
                value = nt_dot(rows, weight[:, c * W : (c + 1) * W])
                acc[at, :] = value if c == 0 else acc[at, :] + value
            return carry

        lax.fori_loop(0, 2, part, 0)

    def activate(m):
        step_rows = 64
        e_me = 4 * g + z // 2
        gate_lane = lax.broadcasted_iota(jnp.int32, (step_rows, EXTRA), 1)

        def part(i, carry):
            at = pl.ds(pl.multiple_of(i * step_rows, step_rows), step_rows)
            a, b, q = a_acc[at, :], b_acc[at, :], q_acc[at, :]
            sig = 0.5 * jnp.tanh(0.5 * a) + 0.5
            silu = a * sig
            qs = q * silu
            gate = jnp.sum(qs * b, axis=1, keepdims=True)
            da_buf[at, :] = (q * b * sig * (1.0 + a * (1.0 - sig))).astype(BF16)
            db_buf[at, :] = qs.astype(BF16)
            extra = jnp.where(gate_lane == e_me, gate, 0.0).astype(BF16)
            n = step_rows // TOK
            sent_wide[m, pl.ds(i * n, n), :, W:] = extra.reshape(n, TOK, EXTRA)
            return carry

        lax.fori_loop(0, ROWS // step_rows, part, 0)

    def send_back(m, c):
        blocks = NG // 2

        def part(i, carry):
            at = pl.ds(pl.multiple_of(i * blocks * TOK, blocks * TOK), blocks * TOK)
            cols = slice(c * W, (c + 1) * W)
            u = jnp.dot(da_buf[at, :], wg[:, cols], preferred_element_type=F32)
            u = u + jnp.dot(db_buf[at, :], wu[:, cols], preferred_element_type=F32)
            back_out[c][m, pl.ds(i * blocks, blocks), :, :W] = u.astype(BF16).reshape(blocks, TOK, W)
            return carry

        lax.fori_loop(0, 2, part, 0)
        fan_out(back_out[c].at[m], came_back[c].at[m], r_ss.at[m, c], r_rs.at[m, c])

    def combine(m, c):
        buf = came_back[c]
        drained(buf.at[m], r_rs.at[m, c])
        rows = buf[m].reshape(ROWS, WIDE[c])
        half = ALL // 2

        def part(i, carry):
            at = pl.ds(pl.multiple_of(i * half, half), half)
            n = half // TOK
            value = jnp.dot(cmat[m, at, :], rows[:, :W], preferred_element_type=F32)
            sums[c][pl.ds(i * n, n), :, :W] = value.reshape(n, TOK, W)
            if c == 1:
                extra = jnp.dot(mmat[m, at, :], rows[:, W:], preferred_element_type=F32)
                sums[c][pl.ds(i * n, n), :, W:] = extra.reshape(n, TOK, EXTRA)
            return carry

        lax.fori_loop(0, 2, part, 0)

    def scatter_item(m, c):
        nr, nl = STEPS[c]
        width = WIDE[c]

        def buf(ref, slot):
            return ref.at[m, c, slot, :, pl.ds(0, width)]

        def hop(direction, s):
            slot, device = (s, up) if direction == 0 else (nr + s, down)
            return remote(
                buf(rs_send, slot), buf(rs_recv, slot), rs_ss.at[m, c, slot], rs_rs.at[m, c, slot], device
            )

        def step(s):
            for direction, count in ((0, nr), (1, nl)):
                if s >= 1 and s - 1 < count:
                    hop(direction, s - 1).wait_recv()
                if s < count:
                    slot = s if direction == 0 else nr + s
                    dest = lax.rem(z + nr - s, NZ) if direction == 0 else lax.rem(z - nl + s + NZ, NZ)
                    value = sums[c][dest]
                    if s >= 1:
                        value = value + rs_recv[m, c, slot - 1, :, :width].astype(F32)
                    rs_send[m, c, slot, :, :width] = value.astype(BF16)
                    copy = hop(direction, s)
                    copy.start()
                    waits.append(copy)

        return step, max(nr, nl) + 1

    def finish(m):
        for c in range(HALVES):
            nr, nl = STEPS[c]
            width = WIDE[c]
            total = sums[c][z]
            total += rs_recv[m, c, nr - 1, :, :width].astype(F32)
            total += rs_recv[m, c, nr + nl - 1, :, :width].astype(F32)
            cols = slice(c * W, (c + 1) * W)
            value = (own_grad[m, :, cols].astype(F32) + total[:, :W]).astype(BF16)
            out_ref[m, :, cols] = value
            if m == 0:
                finished[:, cols] = value
            if c == 1:
                extra = total[:, W:]
                ids = ids_ref[m]
                gates = [
                    jnp.sum(jnp.where(lane == ids[:, k : k + 1], extra, 0.0), axis=1, keepdims=True)
                    for k in range(ids.shape[1])
                ]
                gate_ref[m] = jnp.concatenate(gates, axis=1).astype(BF16)

    def run(items):
        order = sorted((i + 2 * s, i, s) for i, (_, n) in enumerate(items) for s in range(n))
        done = []
        for _, i, s in order:
            items[i][0](s)
            if s == items[i][1] - 1:
                done.append(i)
        return done

    place_own(0, 0)
    place_own(1, 0)
    place_own(0, 1)
    meta_item = ring_items(meta.at[z], lambda o: meta.at[o], meta_ss, meta_rs, STEPS[0])
    first = [meta_item] + [gather_item(k, 0, c) for k in range(2) for c in range(HALVES)]
    order = sorted((i + 2 * s, i, s) for i, (_, n) in enumerate(first) for s in range(n))
    for _, i, s in order:
        first[i][0](s)
        if s == first[i][1] - 1:
            if i == 0:
                build_maps()
            else:
                dispatch((i - 1) // HALVES, 0, (i - 1) % HALVES)
    run([gather_item(0, 1, c) for c in range(HALVES)])
    loads[0].wait()
    loads[1].wait()
    for c in range(HALVES):
        project(0, 0, c, ((wg, a_acc), (wu, b_acc)))
    loads[2].wait()
    for c in range(HALVES):
        project(1, 0, c, ((wd, q_acc),))
    activate(0)
    for c in range(HALVES):
        send_back(0, c)
    for c in range(HALVES):
        dispatch(0, 1, c)
    for c in range(HALVES):
        combine(0, c)
    run([scatter_item(0, c) for c in range(HALVES)])
    finish(0)
    hand = remote(finished, passed, pass_ss, pass_rs, partner)
    hand.start()
    hand.wait()
    own_grad[1] = jnp.where(is_last, og_ref[1].astype(F32), passed[...].astype(F32)).astype(BF16)
    place_own(1, 1)
    second = [gather_item(1, 1, c) for c in range(HALVES)]
    order = sorted((i + 2 * s, i, s) for i, (_, n) in enumerate(second) for s in range(n))
    for _, i, s in order:
        second[i][0](s)
        if s == second[i][1] - 1:
            dispatch(1, 1, i)
    for c in range(HALVES):
        project(0, 1, c, ((wg, a_acc), (wu, b_acc)))
    for c in range(HALVES):
        project(1, 1, c, ((wd, q_acc),))
    activate(1)
    for c in range(HALVES):
        send_back(1, c)
    for c in range(HALVES):
        combine(1, c)
    run([scatter_item(1, c) for c in range(HALVES)])
    finish(1)
    for copy in waits:
        copy.wait_send()
    for m in range(2):
        for c in range(HALVES):
            for kind in range(2):
                drained(picked.at[kind, m, c], x_ss.at[kind, m, c])
            drained(back_out[c].at[m], r_ss.at[m, c])


def local(og, cg, xin, ids, prob, gate_weight, up_weight, down_weight):
    vmem = pl.BlockSpec(memory_space=pltpu.VMEM)
    hbm = pl.BlockSpec(memory_space=pl.ANY)
    dma = pltpu.SemaphoreType.DMA
    out, gate = pl.pallas_call(
        kernel,
        out_shape=(
            jax.ShapeDtypeStruct((2, TOK, D), BF16),
            jax.ShapeDtypeStruct((2, TOK, ids.shape[-1]), BF16),
        ),
        in_specs=[vmem] * 5 + [hbm] * 3,
        out_specs=(vmem, vmem),
        scratch_shapes=[
            pltpu.VMEM((HALF, D), BF16),
            pltpu.VMEM((HALF, D), BF16),
            pltpu.VMEM((HALF, D), BF16),
            pltpu.VMEM((NZ, 2, TOK, EXTRA), BF16),
            pltpu.VMEM((2, TOK, D), BF16),
            pltpu.VMEM((TOK, D), BF16),
            pltpu.VMEM((TOK, D), BF16),
            pltpu.VMEM((2, 2, HALVES, NZ, TOK, W), BF16),
            pltpu.VMEM((2, 2, HALVES, NG, TOK, W), BF16),
            pltpu.VMEM((2, 2, HALVES, NG, TOK, W), BF16),
            pltpu.VMEM((2, NG, TOK, WIDE[0]), BF16),
            pltpu.VMEM((2, NG, TOK, WIDE[0]), BF16),
            pltpu.VMEM((2, NG, TOK, WIDE[1]), BF16),
            pltpu.VMEM((2, NG, TOK, WIDE[1]), BF16),
            pltpu.VMEM((ROWS, HALF), F32),
            pltpu.VMEM((ROWS, HALF), F32),
            pltpu.VMEM((ROWS, HALF), F32),
            pltpu.VMEM((ROWS, HALF), BF16),
            pltpu.VMEM((ROWS, HALF), BF16),
            pltpu.VMEM((2, ROWS, ALL), BF16),
            pltpu.VMEM((2, ALL, ROWS), BF16),
            pltpu.VMEM((2, ALL, ROWS), BF16),
            pltpu.VMEM((NZ, TOK, WIDE[0]), F32),
            pltpu.VMEM((NZ, TOK, WIDE[1]), F32),
            pltpu.VMEM((2, HALVES, NZ - 1, TOK, WIDE[1]), BF16),
            pltpu.VMEM((2, HALVES, NZ - 1, TOK, WIDE[1]), BF16),
            dma((3,)),
            dma((NZ - 1,)),
            dma((NZ - 1,)),
            dma((2, 2, HALVES, NZ - 1)),
            dma((2, 2, HALVES, NZ - 1)),
            dma((2, 2, HALVES)),
            dma((2, 2, HALVES)),
            dma((2, HALVES)),
            dma((2, HALVES)),
            dma((2, HALVES, NZ - 1)),
            dma((2, HALVES, NZ - 1)),
            dma,
            dma,
        ],
        compiler_params=pltpu.CompilerParams(
            collective_id=0, has_side_effects=True, vmem_limit_bytes=63 * 2**20
        ),
    )(
        og,
        cg,
        xin[0],
        ids[0],
        prob[0],
        gate_weight[0, 0].T,
        up_weight[0, 0].T,
        down_weight[0, 0],
    )
    return out[None], gate[None]


def solution(mesh):
    rows = ("group", "local")
    return jax.shard_map(
        local,
        mesh=mesh,
        in_specs=(
            P(None, rows, None),
            P(rows, None),
            P("pipe", None, rows, None),
            P("pipe", None, rows, None),
            P("pipe", None, rows, None),
            P("pipe", rows, None, None),
            P("pipe", rows, None, None),
            P("pipe", rows, None, None),
        ),
        out_specs=(P("pipe", None, rows, None), P("pipe", None, rows, None)),
        check_vma=False,
    )
```

profile of v0, /device:TPU:8, one launch (start us, length us, event | category | flops | bytes accessed | tf_op | source)
XLA Modules:
  0.0 228.3 jit_solution(5803548625711292435)
XLA Ops:
  0.6 1.4 copy.11
  2.0 1.4 copy.10
  3.4 221.9 %shard_map.95 = (bf16[2,32,2048]{2,1,0:T(8,128)(2,1)}, bf16[2,32,6]{2,1,0:T(8,128)(2,1)}) custom-call(bf16[2,32,2048]{2,1,0:T(8,128)(2,1)} %og_ref.1, bf16[32,2048]{1,0:T(8,128)(2,1)} %cg_ref.1, bf16[2,32,2048]{2,1,0:T(8,128)(2,1)} %bitcast.15, s32[2,32,6]{2,1,0:T(8,128)} %bitcast.17, bf16[2,32,6]{2,1,0:T(8,128)(2,1)} %bitcast.18, ...), custom_call_target="tpu_custom_call" | custom-call | tf_op jit(solution)/shard_map/pallas_call | solution.py:375
  225.3 1.4 copy.12
  226.7 1.7 copy.14
where the time goes:
time: 229 us; the launch traced here: 228 us
  Pallas kernels  222 us (97%)
  local copies, waits for them, and re-layouts  5.82 us (3%)
    pallas_call x1, Pallas kernels, local(): pl.pallas_call(kernel, out_shape=(jax.ShapeDtypeStruct((2, TOK, D), BF16)...  222 us
    unnamed x4, local copies, waits for them, and re-layouts  5.82 us

commit v1 on v0

v1 whole, which is shorter than its diff:
```python
import functools

import jax
import jax.numpy as jnp
from jax import lax
from jax.experimental import pallas as pl
from jax.experimental.pallas import tpu as pltpu
from jax.sharding import PartitionSpec as P

MESH = pl.DeviceIdType.MESH
NX, NY, NZ = 4, 4, 8
NG = NX * NY
TOK, D, HALF, SLOTS = 32, 2048, 704, 4
ROWS = NG * TOK
ALL = NZ * TOK
HALVES = 2
W = D // HALVES
EXTRA = 128
WIDE = (W, W + EXTRA)
STEPS = ((4, 3), (3, 4))
NT = (((1,), (1,)), ((), ()))
F32, BF16 = jnp.float32, jnp.bfloat16


def nt_dot(a, b):
    return lax.dot_general(a, b, NT, preferred_element_type=F32)


def kernel(
    og_ref, cg_ref, xin_ref, ids_ref, pr_ref, wg_hbm, wu_hbm, wd_hbm,
    out_ref, gate_ref,
    wg, wu, wd, meta, own_grad, passed, finished,
    gathered, x_picked, x_arrived, g_picked, g_arrived,
    back0, back1, came0, came1,
    a_acc, b_acc, q_acc, da_buf, db_buf, xmat, dmat, cmat, mmat, p0, p1, rs_send, rs_recv,
    w_sem, meta_ss, meta_rs, ag_ss, ag_rs, x_ss, x_rs, f_ss, f_rs, g_ss, g_rs,
    r_ss, r_rs, rs_ss, rs_rs, pass_ss, pass_rs,
):
    pipe = lax.axis_index("pipe")
    g = lax.axis_index("group")
    z = lax.axis_index("local")
    x, y = g // NY, g % NY
    side = z % 2
    base = z - side
    expert = 4 * g + z // 2
    up = (pipe, g, lax.rem(z + 1, NZ))
    down = (pipe, g, lax.rem(z + NZ - 1, NZ))
    mate = (pipe, g, z + 1 - 2 * side)
    partner = (1 - pipe, g, z)
    back, came, sums = (back0, back1), (came0, came1), (p0, p1)
    is_even, is_odd = side == 0, side == 1
    first, last = pipe == 0, pipe == 1
    top = ids_ref.shape[0]
    closing = []

    def remote(src, dst, ss, rs, device):
        return pltpu.make_async_remote_copy(
            src_ref=src, dst_ref=dst, send_sem=ss, recv_sem=rs, device_id=device, device_id_type=MESH
        )

    loads = []
    for i, (h, v) in enumerate(((wg_hbm, wg), (wu_hbm, wu), (wd_hbm, wd))):
        load = pltpu.make_async_copy(h, v, w_sem.at[i])
        load.start()
        loads.append(load)

    barrier = pltpu.get_barrier_semaphore()

    def plane_peer(i):
        dx = i % NX
        dy = lax.rem(i // NX - dx + NY, NY)
        return lax.rem(x + dx, NX) * NY + lax.rem(y + dy, NY)

    def greet(i, carry):
        pl.semaphore_signal(barrier, inc=1, device_id=(pipe, plane_peer(i), z), device_id_type=MESH)
        return carry

    for device in (up, down, partner):
        pl.semaphore_signal(barrier, inc=1, device_id=device, device_id_type=MESH)
    lax.fori_loop(1, NG, greet, 0)

    lane = lax.broadcasted_iota(jnp.int32, (TOK, EXTRA), 1)
    i0 = lax.broadcasted_iota(jnp.int32, (TOK, TOK), 0)
    i1 = lax.broadcasted_iota(jnp.int32, (TOK, TOK), 1)
    lower = (i0 > i1).astype(BF16)
    same = (i0 == i1).astype(BF16)

    def columns(ref, m):
        rows = jnp.concatenate([ref[k, pl.ds(m, 1), :].astype(F32) for k in range(top)], axis=0)
        return nt_dot(same, rows.astype(BF16))

    ids = [columns(ids_ref, m).astype(jnp.int32) for m in range(2)]
    for m in range(2):
        probs = columns(pr_ref, m)
        chosen = jnp.zeros((TOK, EXTRA), F32)
        weight = jnp.zeros((TOK, EXTRA), F32)
        for k in range(top):
            chosen += (lane == ids[m][:, k : k + 1]).astype(F32)
            weight += jnp.where(lane == ids[m][:, k : k + 1] + 64, probs[:, k : k + 1], 0.0)
        before = jnp.dot(lower, chosen.astype(BF16), preferred_element_type=F32)
        meta[z, m] = (chosen * (before + 1.0) + weight).astype(BF16)
    own_grad[0] = jnp.where(last, og_ref[0].astype(F32), cg_ref[...].astype(F32)).astype(BF16)

    def place_own(kind, m):
        src = xin_ref[m] if kind == 0 else own_grad[m]
        for c in range(HALVES):
            gathered[kind, m, c, z] = src[:, c * W : (c + 1) * W]

    place_own(0, 0)
    place_own(1, 0)
    place_own(0, 1)
    pl.semaphore_wait(barrier, NG - 1 + 3)

    def run(items, hooks=None):
        lead = 2 if hooks and len(items) > 2 else 0
        order = sorted(((i if i or not lead else -lead) + 2 * s, i, s) for i, (_, n) in enumerate(items) for s in range(n))
        for _, i, s in order:
            items[i][0](s)
            if hooks and s == items[i][1] - 1:
                hooks[i]()

    def ring(own, at, ss, rs, counts):
        nr, nl = counts

        def hop(direction, s):
            if direction == 0:
                origin, device, slot = lax.rem(z - s + NZ, NZ), up, s
            else:
                origin, device, slot = lax.rem(z + s, NZ), down, nr + s
            return remote(own if s == 0 else at(origin), at(origin), ss.at[slot], rs.at[slot], device)

        def step(s):
            for direction, count in ((0, nr), (1, nl)):
                if s >= 1 and s - 1 < count:
                    hop(direction, s - 1).wait_recv()
                if s < count:
                    hop(direction, s).start()

        for direction, count in ((0, nr), (1, nl)):
            for s in range(count):
                closing.append(lambda d=direction, s=s: hop(d, s).wait_send())
        return step, max(nr, nl) + 1

    def half_ring(own, at, ss, rs):
        def hop(direction, s):
            if direction == 0:
                origin, device, slot = lax.rem(z - s + NZ, NZ), up, s
            else:
                origin, device, slot = lax.rem(z + s, NZ), down, 3 + s
            return remote(own if s == 0 else at(origin), at(origin), ss.at[slot], rs.at[slot], device)

        def step(s):
            for direction in range(2):
                sends, takes = (is_odd, is_even) if direction == 0 else (is_even, is_odd)
                if s in (1, 2):
                    hop(direction, s - 1).wait_recv()
                if s == 3:
                    pl.when(takes)(lambda: hop(direction, 2).wait_recv())
                if s < 2:
                    hop(direction, s).start()
                if s == 2:
                    pl.when(sends)(lambda: hop(direction, 2).start())

        for direction in range(2):
            for s in range(2):
                closing.append(lambda d=direction, s=s: hop(d, s).wait_send())
            sends = is_odd if direction == 0 else is_even
            closing.append(lambda d=direction, k=sends: pl.when(k)(lambda: hop(d, 2).wait_send()))
        return step, 4

    def gather(kind, m, c):
        src = (xin_ref if kind == 0 else own_grad).at[m, :, pl.ds(c * W, W)]
        at = lambda o: gathered.at[kind, m, c, o]
        ss, rs = ag_ss.at[kind, m, c], ag_rs.at[kind, m, c]
        return half_ring(src, at, ss, rs) if kind == 0 else ring(src, at, ss, rs, STEPS[c])

    def fan_out(src, dst, ss, rs):
        def send(i, carry):
            peer = plane_peer(i)
            remote(src(peer), dst(g), ss, rs, (pipe, peer, z)).start()
            return carry

        lax.fori_loop(1, NG, send, 0)

    def drain(ref, sem):
        pltpu.make_async_copy(ref, ref, sem).wait()

    def origin_of(order):
        return lax.rem(base - 3 + NZ + order, NZ)

    def iota(shape, dim):
        return lax.broadcasted_iota(jnp.int32, shape, dim)

    def build_x_maps():
        hr = TOK // 2
        sel = (iota((NG * hr, EXTRA), 1) == iota((NG * hr, EXTRA), 0) // hr * 4 + z // 2).astype(BF16)
        r, t = iota((NG * hr, ALL // 2), 0), iota((NG * hr, ALL // 2), 1)
        want = jnp.where(r % hr // SLOTS == t // TOK, r % SLOTS + 1, -1).astype(F32)
        for m in range(2):
            near = jnp.concatenate([meta[origin_of(4 * side + j), m] for j in range(4)], axis=0)
            xmat[m] = (nt_dot(sel, near) == want).astype(BF16)

    def build_maps():
        e_lane = iota((ROWS, EXTRA), 1)
        e_row = iota((ROWS, EXTRA), 0) // TOK * 4 + z // 2
        sel_slot = (e_lane == e_row).astype(BF16)
        sel_prob = (e_lane == e_row + 64).astype(BF16)
        r, t = iota((ROWS, ALL), 0), iota((ROWS, ALL), 1)
        want0 = jnp.where(origin_of(r % TOK // SLOTS) == t // TOK, r % SLOTS + 1, -1).astype(F32)
        r, t = iota((ALL, ROWS), 1), iota((ALL, ROWS), 0)
        want1 = jnp.where(origin_of(r % TOK // SLOTS) == t // TOK, r % SLOTS + 1, -1).astype(F32)
        for m in range(2):
            table = meta[:, m].reshape(ALL, EXTRA)
            dmat[m] = (nt_dot(sel_slot, table) == want0).astype(BF16)
            hit = nt_dot(table, sel_slot) == want1
            mmat[m] = hit.astype(BF16)
            cmat[m] = jnp.where(hit, nt_dot(table, sel_prob), 0.0).astype(BF16)

    my_half = pl.ds(pl.multiple_of(side * (TOK // 2), TOK // 2), TOK // 2)

    def dispatch_x(m, c):
        tokens = jnp.concatenate([gathered[0, m, c, origin_of(4 * side + j)] for j in range(4)], axis=0)
        rows = jnp.dot(xmat[m], tokens, preferred_element_type=F32).astype(BF16)
        x_picked[m, c] = rows.reshape(NG, TOK // 2, W)
        fan_out(
            lambda peer: x_picked.at[m, c, peer],
            lambda col: x_arrived.at[m, c, col, my_half, :],
            x_ss.at[m, c],
            x_rs.at[m, c],
        )
        x_arrived[m, c, g, my_half, :] = x_picked[m, c, g]

    def forward(m, c):
        block = x_arrived.at[m, c, :, my_half, :]
        return remote(block, block, f_ss.at[m, c], f_rs.at[m, c], mate)

    def forward_x(m, c):
        drain(x_picked.at[m, c, pl.ds(0, NG - 1)], x_rs.at[m, c])
        forward(m, c).start()

    def dispatch_g(m, c):
        tokens = gathered[1, m, c].reshape(ALL, W)
        rows = jnp.dot(dmat[m], tokens, preferred_element_type=F32).astype(BF16)
        g_picked[m, c] = rows.reshape(NG, TOK, W)
        fan_out(
            lambda peer: g_picked.at[m, c, peer],
            lambda col: g_arrived.at[m, c, col],
            g_ss.at[m, c],
            g_rs.at[m, c],
        )
        g_arrived[m, c, g] = g_picked[m, c, g]

    def project(rows_ref, c, pairs):
        rows = rows_ref[...].reshape(ROWS, W)
        for weight, acc in pairs:
            value = nt_dot(rows, weight[:, c * W : (c + 1) * W])
            acc[...] = value if c == 0 else acc[...] + value

    def project_x(m, c):
        forward(m, c).wait_recv()
        project(x_arrived.at[m, c], c, ((wg, a_acc), (wu, b_acc)))

    def project_g(m, c):
        drain(g_arrived.at[m, c, pl.ds(0, NG - 1)], g_rs.at[m, c])
        project(g_arrived.at[m, c], c, ((wd, q_acc),))

    def activate(m):
        step_rows = 128
        gate_lane = iota((step_rows, EXTRA), 1)

        def part(i, carry):
            at = pl.ds(pl.multiple_of(i * step_rows, step_rows), step_rows)
            a, b, q = a_acc[at, :], b_acc[at, :], q_acc[at, :]
            sig = 0.5 * jnp.tanh(0.5 * a) + 0.5
            silu = a * sig
            qs = q * silu
            gate = jnp.sum(qs * b, axis=1, keepdims=True)
            da_buf[at, :] = (q * b * sig * (1.0 + a * (1.0 - sig))).astype(BF16)
            db_buf[at, :] = qs.astype(BF16)
            extra = jnp.where(gate_lane == expert, gate, 0.0).astype(BF16)
            n = step_rows // TOK
            back1[m, pl.ds(i * n, n), :, W:] = extra.reshape(n, TOK, EXTRA)
            return carry

        lax.fori_loop(0, ROWS // step_rows, part, 0)

    def send_back(m, c):
        cols = slice(c * W, (c + 1) * W)
        u = jnp.dot(da_buf[...], wg[:, cols], preferred_element_type=F32)
        u = u + jnp.dot(db_buf[...], wu[:, cols], preferred_element_type=F32)
        back[c][m, :, :, :W] = u.astype(BF16).reshape(NG, TOK, W)
        fan_out(
            lambda peer: back[c].at[m, peer], lambda col: came[c].at[m, col], r_ss.at[m, c], r_rs.at[m, c]
        )
        came[c][m, g] = back[c][m, g]

    def combine(m, c):
        drain(came[c].at[m, pl.ds(0, NG - 1)], r_rs.at[m, c])
        rows = came[c][m].reshape(ROWS, WIDE[c])
        value = jnp.dot(cmat[m], rows[:, :W], preferred_element_type=F32)
        sums[c][:, :, :W] = value.reshape(NZ, TOK, W)
        if c == 1:
            extra = jnp.dot(mmat[m], rows[:, W:], preferred_element_type=F32)
            sums[c][:, :, W:] = extra.reshape(NZ, TOK, EXTRA)

    def scatter(m, c):
        nr, nl = STEPS[c]
        width = WIDE[c]

        def buf(ref, slot):
            return ref.at[m, c, slot, :, pl.ds(0, width)]

        def hop(direction, s):
            slot, device = (s, up) if direction == 0 else (nr + s, down)
            return remote(
                buf(rs_send, slot), buf(rs_recv, slot), rs_ss.at[m, c, slot], rs_rs.at[m, c, slot], device
            )

        def step(s):
            for direction, count in ((0, nr), (1, nl)):
                if s >= 1 and s - 1 < count:
                    hop(direction, s - 1).wait_recv()
                if s < count:
                    slot = s if direction == 0 else nr + s
                    dest = lax.rem(z + nr - s, NZ) if direction == 0 else lax.rem(z - nl + s + NZ, NZ)
                    value = sums[c][dest]
                    if s >= 1:
                        value = value + rs_recv[m, c, slot - 1, :, :width].astype(F32)
                    rs_send[m, c, slot, :, :width] = value.astype(BF16)
                    hop(direction, s).start()

        def close():
            for direction, count in ((0, nr), (1, nl)):
                for s in range(count):
                    hop(direction, s).wait_send()

        return (step, max(nr, nl) + 1), close

    def finish(m):
        for c in range(HALVES):
            nr, nl = STEPS[c]
            width = WIDE[c]
            total = sums[c][z]
            total += rs_recv[m, c, nr - 1, :, :width].astype(F32)
            total += rs_recv[m, c, nr + nl - 1, :, :width].astype(F32)
            cols = slice(c * W, (c + 1) * W)
            value = (own_grad[m, :, cols].astype(F32) + total[:, :W]).astype(BF16)
            out_ref[m, :, cols] = value
            if m == 0:
                finished[:, cols] = value
            if c == 1:
                extra = total[:, W:]
                gates = jnp.zeros((TOK, EXTRA), F32)
                for k in range(top):
                    picked = jnp.sum(jnp.where(lane == ids[m][:, k : k + 1], extra, 0.0), axis=1, keepdims=True)
                    gates += jnp.where(lane == k, picked, 0.0)
                flat = lax.dot_general(
                    gates.astype(BF16), same, (((0,), (0,)), ((), ())), preferred_element_type=F32
                ).astype(BF16)
                for k in range(top):
                    gate_ref[k, pl.ds(m, 1), :] = flat[k : k + 1, :]

    def collect(m):
        for c in range(HALVES):
            combine(m, c)
        run([scatter(m, c)[0] for c in range(HALVES)])
        finish(m)

    both = range(HALVES)
    handed = lambda: remote(finished, passed, pass_ss, pass_rs, partner)
    late = [gather(1, 1, c) for c in both]

    def late_gradients():
        place_own(1, 1)
        run(late, [lambda c=c: dispatch_g(1, c) for c in both])

    def early_part(c):
        dispatch_g(0, c)
        forward_x(0, c)

    items = [ring(meta.at[z], lambda o: meta.at[o], meta_ss, meta_rs, STEPS[0])]
    items += [gather(0, 0, c) for c in both] + [gather(1, 0, c) for c in both] + [gather(0, 1, c) for c in both]
    def second_x():
        dispatch_x(0, 1)
        build_maps()

    hooks = [build_x_maps, lambda: dispatch_x(0, 0), second_x]
    hooks += [lambda c=c: early_part(c) for c in both]
    hooks += [lambda: None] * 2
    run(items, hooks)

    @pl.when(first)
    def _():
        for c in both:
            dispatch_x(1, c)

    loads[0].wait()
    loads[1].wait()
    for c in both:
        project_x(0, c)
    loads[2].wait()
    for c in both:
        project_g(0, c)
    activate(0)
    for c in both:
        send_back(0, c)

    @pl.when(last)
    def _():
        own_grad[1] = og_ref[1]
        for c in both:
            dispatch_x(1, c)
        late_gradients()
        collect(0)
        handed().start()
        for c in both:
            forward_x(1, c)
        handed().wait_send()

    @pl.when(first)
    def _():
        for c in both:
            forward_x(1, c)
        handed().wait_recv()
        own_grad[1] = passed[...]
        late_gradients()
        collect(0)

    for c in both:
        project_x(1, c)
    for c in both:
        project_g(1, c)
    activate(1)
    for c in both:
        send_back(1, c)
    collect(1)

    for close in closing:
        close()
    for m in range(2):
        for c in both:
            scatter(m, c)[1]()
            forward(m, c).wait_send()
            drain(x_picked.at[m, c, pl.ds(0, NG - 1)], x_ss.at[m, c])
            drain(g_picked.at[m, c, pl.ds(0, NG - 1)], g_ss.at[m, c])
            drain(back[c].at[m, pl.ds(0, NG - 1)], r_ss.at[m, c])


def local(og, cg, xin, ids, prob, gate_weight, up_weight, down_weight):
    vmem = pl.BlockSpec(memory_space=pltpu.VMEM)
    hbm = pl.BlockSpec(memory_space=pl.ANY)
    dma = pltpu.SemaphoreType.DMA
    top = ids.shape[-1]
    both = (2, HALVES)
    hops = (NZ - 1,)
    out, gate = pl.pallas_call(
        kernel,
        out_shape=(
            jax.ShapeDtypeStruct((2, TOK, D), BF16),
            jax.ShapeDtypeStruct((top, 2, TOK), BF16),
        ),
        in_specs=[vmem] * 5 + [hbm] * 3,
        out_specs=(vmem, vmem),
        scratch_shapes=[
            pltpu.VMEM((HALF, D), BF16),
            pltpu.VMEM((HALF, D), BF16),
            pltpu.VMEM((HALF, D), BF16),
            pltpu.VMEM((NZ, 2, TOK, EXTRA), BF16),
            pltpu.VMEM((2, TOK, D), BF16),
            pltpu.VMEM((TOK, D), BF16),
            pltpu.VMEM((TOK, D), BF16),
            pltpu.VMEM((2, *both, NZ, TOK, W), BF16),
            pltpu.VMEM((*both, NG, TOK // 2, W), BF16),
            pltpu.VMEM((*both, NG, TOK, W), BF16),
            pltpu.VMEM((*both, NG, TOK, W), BF16),
            pltpu.VMEM((*both, NG, TOK, W), BF16),
            pltpu.VMEM((2, NG, TOK, WIDE[0]), BF16),
            pltpu.VMEM((2, NG, TOK, WIDE[1]), BF16),
            pltpu.VMEM((2, NG, TOK, WIDE[0]), BF16),
            pltpu.VMEM((2, NG, TOK, WIDE[1]), BF16),
            pltpu.VMEM((ROWS, HALF), F32),
            pltpu.VMEM((ROWS, HALF), F32),
            pltpu.VMEM((ROWS, HALF), F32),
            pltpu.VMEM((ROWS, HALF), BF16),
            pltpu.VMEM((ROWS, HALF), BF16),
            pltpu.VMEM((2, ROWS // 2, ALL // 2), BF16),
            pltpu.VMEM((2, ROWS, ALL), BF16),
            pltpu.VMEM((2, ALL, ROWS), BF16),
            pltpu.VMEM((2, ALL, ROWS), BF16),
            pltpu.VMEM((NZ, TOK, WIDE[0]), F32),
            pltpu.VMEM((NZ, TOK, WIDE[1]), F32),
            pltpu.VMEM((*both, NZ - 1, TOK, WIDE[1]), BF16),
            pltpu.VMEM((*both, NZ - 1, TOK, WIDE[1]), BF16),
            dma((3,)),
            dma(hops),
            dma(hops),
            dma((2, *both, *hops)),
            dma((2, *both, *hops)),
        ]
        + [dma(both)] * 8
        + [dma((*both, *hops))] * 2
        + [dma] * 2,
        compiler_params=pltpu.CompilerParams(
            collective_id=0, has_side_effects=True, vmem_limit_bytes=63 * 2**20
        ),
    )(
        og,
        cg,
        xin[0],
        jnp.transpose(ids[0], (2, 0, 1)),
        jnp.transpose(prob[0], (2, 0, 1)),
        gate_weight[0, 0].T,
        up_weight[0, 0].T,
        down_weight[0, 0],
    )
    return out[None], jnp.transpose(gate, (1, 2, 0))[None]


def solution(mesh):
    rows = ("group", "local")
    return jax.shard_map(
        local,
        mesh=mesh,
        in_specs=(
            P(None, rows, None),
            P(rows, None),
            P("pipe", None, rows, None),
            P("pipe", None, rows, None),
            P("pipe", None, rows, None),
            P("pipe", rows, None, None),
            P("pipe", rows, None, None),
            P("pipe", rows, None, None),
        ),
        out_specs=(P("pipe", None, rows, None), P("pipe", None, rows, None)),
        check_vma=False,
    )
```

time: 229 us -> 193 us (0.84)
  Pallas kernels: 222 us -> 188 us
  local copies, waits for them, and re-layouts: 5.82 us -> 2.92 us
    pallas_call x1, Pallas kernels: 222 us -> 188 us  [local(): pl.pallas_call(kernel, out_shape=(jax.ShapeDtypeStruct((2, TOK, D), BF16)...]
    unnamed x4 -> x2, local copies, waits for them, and re-layouts: 5.82 us -> 2.92 us
where the time goes in v1:
time: 193 us; the launch traced here: 192 us
  Pallas kernels  188 us (97%)
  local copies, waits for them, and re-layouts  2.92 us (2%)
    pallas_call x1, Pallas kernels, local(): pl.pallas_call(kernel, out_shape=(jax.ShapeDtypeStruct((2, TOK, D), BF16)...  188 us

profile of v1, /device:TPU:8, one launch (start us, length us, event | category | flops | bytes accessed | tf_op | source)
XLA Modules:
  0.0 191.6 jit_solution(7816794273563224489)
XLA Ops:
  0.6 188.0 %shard_map.95 = (bf16[2,32,2048]{2,1,0:T(8,128)(2,1)}, bf16[6,2,32]{2,1,0:T(2,128)(2,1)}) custom-call(bf16[2,32,2048]{2,1,0:T(8,128)(2,1)} %og_ref.1, bf16[32,2048]{1,0:T(8,128)(2,1)} %cg_ref.1, bf16[2,32,2048]{2,1,0:T(8,128)(2,1)} %bitcast.21, s32[6,2,32]{2,1,0:T(2,128)} %bitcast.23, bf16[6,2,32]{2,1,0:T(2,128)(2,1)} %bitcast.24, ...), custom_call_target="tpu_custom_call" | custom-call | tf_op jit(solution)/shard_map/pallas_call | solution.py:456
  188.7 1.7 copy.12
  190.4 1.3 copy.13

commit v2 on v1

--- a/solution.py
+++ b/solution.py
@@ -34,7 +34,7 @@
     back0, back1, came0, came1,
     a_acc, b_acc, q_acc, da_buf, db_buf, xmat, dmat, cmat, mmat, p0, p1, rs_send, rs_recv,
     w_sem, meta_ss, meta_rs, ag_ss, ag_rs, x_ss, x_rs, f_ss, f_rs, g_ss, g_rs,
-    r_ss, r_rs, rs_ss, rs_rs, pass_ss, pass_rs,
+    r_ss, r_rs, rs_ss, rs_rs, pass_ss, pass_rs, turn,
 ):
     pipe = lax.axis_index("pipe")
     g = lax.axis_index("group")
@@ -51,7 +51,6 @@
     is_even, is_odd = side == 0, side == 1
     first, last = pipe == 0, pipe == 1
     top = ids_ref.shape[0]
-    closing = []
 
     def remote(src, dst, ss, rs, device):
         return pltpu.make_async_remote_copy(
@@ -61,7 +60,6 @@
     loads = []
     for i, (h, v) in enumerate(((wg_hbm, wg), (wu_hbm, wu), (wd_hbm, wd))):
         load = pltpu.make_async_copy(h, v, w_sem.at[i])
-        load.start()
         loads.append(load)
 
     barrier = pltpu.get_barrier_semaphore()
@@ -111,9 +109,12 @@
     place_own(0, 1)
     pl.semaphore_wait(barrier, NG - 1 + 3)
 
-    def run(items, hooks=None):
-        lead = 2 if hooks and len(items) > 2 else 0
-        order = sorted(((i if i or not lead else -lead) + 2 * s, i, s) for i, (_, n) in enumerate(items) for s in range(n))
+    def run(items, hooks=None, ahead=0, keys=(0, 1, 2, 3), pace=(2,) * 5):
+        order = sorted(
+            (keys[i] + pace[i] * s if s or i >= ahead else i - NZ, i, s)
+            for i, (_, n, _) in enumerate(items)
+            for s in range(n)
+        )
         for _, i, s in order:
             items[i][0](s)
             if hooks and s == items[i][1] - 1:
@@ -136,10 +137,12 @@
                 if s < count:
                     hop(direction, s).start()
 
-        for direction, count in ((0, nr), (1, nl)):
-            for s in range(count):
-                closing.append(lambda d=direction, s=s: hop(d, s).wait_send())
-        return step, max(nr, nl) + 1
+        def close():
+            for direction, count in ((0, nr), (1, nl)):
+                for s in range(count):
+                    hop(direction, s).wait_send()
+
+        return step, max(nr, nl) + 1, close
 
     def half_ring(own, at, ss, rs):
         def hop(direction, s):
@@ -161,18 +164,19 @@
                 if s == 2:
                     pl.when(sends)(lambda: hop(direction, 2).start())
 
-        for direction in range(2):
-            for s in range(2):
-                closing.append(lambda d=direction, s=s: hop(d, s).wait_send())
-            sends = is_odd if direction == 0 else is_even
-            closing.append(lambda d=direction, k=sends: pl.when(k)(lambda: hop(d, 2).wait_send()))
-        return step, 4
-
-    def gather(kind, m, c):
+        def close():
+            for direction in range(2):
+                for s in range(2):
+                    hop(direction, s).wait_send()
+                pl.when(is_odd if direction == 0 else is_even)(lambda: hop(direction, 2).wait_send())
+
+        return step, 4, close
+
+    def gather(kind, m, c, whole):
         src = (xin_ref if kind == 0 else own_grad).at[m, :, pl.ds(c * W, W)]
         at = lambda o: gathered.at[kind, m, c, o]
         ss, rs = ag_ss.at[kind, m, c], ag_rs.at[kind, m, c]
-        return half_ring(src, at, ss, rs) if kind == 0 else ring(src, at, ss, rs, STEPS[c])
+        return ring(src, at, ss, rs, STEPS[c]) if whole else half_ring(src, at, ss, rs)
 
     def fan_out(src, dst, ss, rs):
         def send(i, carry):
@@ -218,37 +222,42 @@
 
     my_half = pl.ds(pl.multiple_of(side * (TOK // 2), TOK // 2), TOK // 2)
 
-    def dispatch_x(m, c):
-        tokens = jnp.concatenate([gathered[0, m, c, origin_of(4 * side + j)] for j in range(4)], axis=0)
+    route = ((x_picked, x_arrived, x_ss, x_rs), (g_picked, g_arrived, g_ss, g_rs))
+
+    def dispatch(kind, m, c):
+        picked, arrived, ss, rs = route[kind]
+        tokens = gathered[kind, m, c].reshape(ALL, W)
+        rows = jnp.dot(dmat[m], tokens, preferred_element_type=F32).astype(BF16)
+        picked[m, c] = rows.reshape(NG, TOK, W)
+        fan_out(
+            lambda peer: picked.at[m, c, peer], lambda col: arrived.at[m, c, col], ss.at[m, c], rs.at[m, c]
+        )
+        arrived[m, c, g] = picked[m, c, g]
+
+    def dispatch_half(kind, m, c):
+        picked, arrived, ss, rs = route[kind]
+        tokens = jnp.concatenate([gathered[kind, m, c, origin_of(4 * side + j)] for j in range(4)], axis=0)
         rows = jnp.dot(xmat[m], tokens, preferred_element_type=F32).astype(BF16)
-        x_picked[m, c] = rows.reshape(NG, TOK // 2, W)
+        picked[m, c, :, : TOK // 2, :] = rows.reshape(NG, TOK // 2, W)
         fan_out(
-            lambda peer: x_picked.at[m, c, peer],
-            lambda col: x_arrived.at[m, c, col, my_half, :],
-            x_ss.at[m, c],
-            x_rs.at[m, c],
+            lambda peer: picked.at[m, c, peer, pl.ds(0, TOK // 2), :],
+            lambda col: arrived.at[m, c, col, my_half, :],
+            ss.at[m, c],
+            rs.at[m, c],
         )
-        x_arrived[m, c, g, my_half, :] = x_picked[m, c, g]
-
-    def forward(m, c):
-        block = x_arrived.at[m, c, :, my_half, :]
-        return remote(block, block, f_ss.at[m, c], f_rs.at[m, c], mate)
-
-    def forward_x(m, c):
-        drain(x_picked.at[m, c, pl.ds(0, NG - 1)], x_rs.at[m, c])
-        forward(m, c).start()
-
-    def dispatch_g(m, c):
-        tokens = gathered[1, m, c].reshape(ALL, W)
-        rows = jnp.dot(dmat[m], tokens, preferred_element_type=F32).astype(BF16)
-        g_picked[m, c] = rows.reshape(NG, TOK, W)
-        fan_out(
-            lambda peer: g_picked.at[m, c, peer],
-            lambda col: g_arrived.at[m, c, col],
-            g_ss.at[m, c],
-            g_rs.at[m, c],
-        )
-        g_arrived[m, c, g] = g_picked[m, c, g]
+        arrived[m, c, g, my_half, :] = picked[m, c, g, : TOK // 2, :]
+
+    def halves(kind, m, c):
+        return route[kind][0].at[m, c, pl.ds(0, NG - 1), pl.ds(0, TOK // 2), :]
+
+    def exchange(kind, m, c, at, count):
+        block = route[kind][1].at[m, c, pl.ds(at, count), my_half, :]
+        return remote(block, block, f_ss.at[kind, m, c], f_rs.at[kind, m, c], mate)
+
+    def forward(kind, m, c):
+        drain(halves(kind, m, c), route[kind][3].at[m, c])
+        for part in range(4):
+            exchange(kind, m, c, part * NG // 4, NG // 4).start()
 
     def project(rows_ref, c, pairs):
         rows = rows_ref[...].reshape(ROWS, W)
@@ -257,11 +266,14 @@
             acc[...] = value if c == 0 else acc[...] + value
 
     def project_x(m, c):
-        forward(m, c).wait_recv()
+        exchange(0, m, c, 0, NG).wait_recv()
         project(x_arrived.at[m, c], c, ((wg, a_acc), (wu, b_acc)))
 
-    def project_g(m, c):
-        drain(g_arrived.at[m, c, pl.ds(0, NG - 1)], g_rs.at[m, c])
+    def project_g(m, c, whole):
+        if whole:
+            drain(g_arrived.at[m, c, pl.ds(0, NG - 1)], g_rs.at[m, c])
+        else:
+            exchange(1, m, c, 0, NG).wait_recv()
         project(g_arrived.at[m, c], c, ((wd, q_acc),))
 
     def activate(m):
@@ -284,11 +296,13 @@
 
         lax.fori_loop(0, ROWS // step_rows, part, 0)
 
-    def send_back(m, c):
+    def backward(m, c):
         cols = slice(c * W, (c + 1) * W)
         u = jnp.dot(da_buf[...], wg[:, cols], preferred_element_type=F32)
         u = u + jnp.dot(db_buf[...], wu[:, cols], preferred_element_type=F32)
         back[c][m, :, :, :W] = u.astype(BF16).reshape(NG, TOK, W)
+
+    def send_back(m, c):
         fan_out(
             lambda peer: back[c].at[m, peer], lambda col: came[c].at[m, col], r_ss.at[m, c], r_rs.at[m, c]
         )
@@ -334,7 +348,7 @@
                 for s in range(count):
                     hop(direction, s).wait_send()
 
-        return (step, max(nr, nl) + 1), close
+        return step, max(nr, nl) + 1, close
 
     def finish(m):
         for c in range(HALVES):
@@ -360,90 +374,125 @@
                 for k in range(top):
                     gate_ref[k, pl.ds(m, 1), :] = flat[k : k + 1, :]
 
-    def collect(m):
+    def collect(m, between=lambda: None):
         for c in range(HALVES):
             combine(m, c)
-        run([scatter(m, c)[0] for c in range(HALVES)])
+        between()
+        run([scatter(m, c) for c in range(HALVES)])
         finish(m)
 
     both = range(HALVES)
     handed = lambda: remote(finished, passed, pass_ss, pass_rs, partner)
-    late = [gather(1, 1, c) for c in both]
-
-    def late_gradients():
-        place_own(1, 1)
-        run(late, [lambda c=c: dispatch_g(1, c) for c in both])
-
-    def early_part(c):
-        dispatch_g(0, c)
-        forward_x(0, c)
+    second_x = [gather(0, 1, c, False) for c in both]
+    half_g = [gather(1, 1, c, False) for c in both]
+    whole_g = [gather(1, 1, c, True) for c in both]
+    send_x = [lambda c=c: dispatch_half(0, 1, c) for c in both]
+    send_half_g = [lambda c=c: dispatch_half(1, 1, c) for c in both]
+    send_whole_g = [lambda c=c: dispatch(1, 1, c) for c in both]
+
+    def release():
+        pl.semaphore_signal(turn, inc=1, device_id=partner, device_id_type=MESH)
 
     items = [ring(meta.at[z], lambda o: meta.at[o], meta_ss, meta_rs, STEPS[0])]
-    items += [gather(0, 0, c) for c in both] + [gather(1, 0, c) for c in both] + [gather(0, 1, c) for c in both]
-    def second_x():
-        dispatch_x(0, 1)
+    items += [gather(kind, 0, c, kind == 1) for kind in range(2) for c in both]
+
+    def rest_of_x():
+        dispatch_half(0, 0, 1)
         build_maps()
 
-    hooks = [build_x_maps, lambda: dispatch_x(0, 0), second_x]
-    hooks += [lambda c=c: early_part(c) for c in both]
-    hooks += [lambda: None] * 2
-    run(items, hooks)
+    hooks = [build_x_maps, lambda: dispatch_half(0, 0, 0), rest_of_x]
+    hooks += [lambda c=c: dispatch(1, 0, c) for c in both]
+    run(items, hooks, 3, (-1, 0, 0.5, 3, 4), (1.4, 2, 2, 2, 2))
+
+    for load in loads:
+        load.start()
 
     @pl.when(first)
     def _():
-        for c in both:
-            dispatch_x(1, c)
-
-    loads[0].wait()
-    loads[1].wait()
+        run(second_x, send_x)
+
+    for c in both:
+        forward(0, 0, c)
+    for load in loads:
+        load.wait()
     for c in both:
         project_x(0, c)
-    loads[2].wait()
     for c in both:
-        project_g(0, c)
+        project_g(0, c, True)
+
+    @pl.when(first)
+    def _():
+        for c in both:
+            forward(0, 1, c)
+
     activate(0)
     for c in both:
-        send_back(0, c)
+        backward(0, c)
+        pl.when(last)(lambda: send_back(0, c))
 
     @pl.when(last)
     def _():
         own_grad[1] = og_ref[1]
-        for c in both:
-            dispatch_x(1, c)
-        late_gradients()
-        collect(0)
+        place_own(1, 1)
+        run(second_x + whole_g, send_x + send_whole_g)
+        collect(0, release)
         handed().start()
         for c in both:
-            forward_x(1, c)
+            forward(0, 1, c)
+        for c in both:
+            project_g(1, c, True)
+        for c in both:
+            project_x(1, c)
         handed().wait_send()
 
     @pl.when(first)
     def _():
-        for c in both:
-            forward_x(1, c)
+        pl.semaphore_wait(turn, 1)
+        for c in both:
+            send_back(0, c)
         handed().wait_recv()
         own_grad[1] = passed[...]
-        late_gradients()
-        collect(0)
-
-    for c in both:
-        project_x(1, c)
-    for c in both:
-        project_g(1, c)
+        place_own(1, 1)
+        run(half_g, send_half_g)
+        for c in both:
+            forward(1, 1, c)
+        for c in both:
+            project_x(1, c)
+        for c in both:
+            project_g(1, c, False)
+
     activate(1)
     for c in both:
+        backward(1, c)
         send_back(1, c)
+
+    @pl.when(first)
+    def _():
+        collect(0)
+
     collect(1)
 
-    for close in closing:
-        close()
-    for m in range(2):
-        for c in both:
-            scatter(m, c)[1]()
-            forward(m, c).wait_send()
-            drain(x_picked.at[m, c, pl.ds(0, NG - 1)], x_ss.at[m, c])
-            drain(g_picked.at[m, c, pl.ds(0, NG - 1)], g_ss.at[m, c])
+    for item in items + second_x + [scatter(m, c) for m in range(2) for c in both]:
+        item[2]()
+    for c in both:
+        for m in range(2):
+            exchange(0, m, c, 0, NG).wait_send()
+            drain(halves(0, m, c), x_ss.at[m, c])
             drain(back[c].at[m, pl.ds(0, NG - 1)], r_ss.at[m, c])
+        drain(g_picked.at[0, c, pl.ds(0, NG - 1)], g_ss.at[0, c])
+
+    @pl.when(first)
+    def _():
+        for c in both:
+            half_g[c][2]()
+            exchange(1, 1, c, 0, NG).wait_send()
+            drain(halves(1, 1, c), g_ss.at[1, c])
+
+    @pl.when(last)
+    def _():
+        for c in both:
+            whole_g[c][2]()
+            drain(g_picked.at[1, c, pl.ds(0, NG - 1)], g_ss.at[1, c])
 
 
 def local(og, cg, xin, ids, prob, gate_weight, up_weight, down_weight):
@@ -470,7 +519,7 @@
             pltpu.VMEM((TOK, D), BF16),
             pltpu.VMEM((TOK, D), BF16),
             pltpu.VMEM((2, *both, NZ, TOK, W), BF16),
-            pltpu.VMEM((*both, NG, TOK // 2, W), BF16),
+            pltpu.VMEM((*both, NG, TOK, W), BF16),
             pltpu.VMEM((*both, NG, TOK, W), BF16),
             pltpu.VMEM((*both, NG, TOK, W), BF16),
             pltpu.VMEM((*both, NG, TOK, W), BF16),
@@ -497,9 +546,12 @@
             dma((2, *both, *hops)),
             dma((2, *both, *hops)),
         ]
-        + [dma(both)] * 8
+        + [dma(both)] * 2
+        + [dma((2, *both))] * 2
+        + [dma(both)] * 4
         + [dma((*both, *hops))] * 2
-        + [dma] * 2,
+        + [dma] * 2
+        + [pltpu.SemaphoreType.REGULAR],
         compiler_params=pltpu.CompilerParams(
             collective_id=0, has_side_effects=True, vmem_limit_bytes=63 * 2**20
         ),

time: 193 us -> 180 us (0.933)
  Pallas kernels: 188 us -> 177 us
    pallas_call x1, Pallas kernels: 188 us -> 177 us  [local(): pl.pallas_call(kernel, out_shape=(jax.ShapeDtypeStruct((2, TOK, D), BF16)...]
where the time goes in v2:
time: 180 us
  Pallas kernels  177 us (98%)
  local copies, waits for them, and re-layouts  2.92 us (2%)
    pallas_call x1, Pallas kernels, local(): pl.pallas_call(kernel, out_shape=(jax.ShapeDtypeStruct((2, TOK, D), BF16)...  177 us

profile of v2, /device:TPU:8, one launch (start us, length us, event | category | flops | bytes accessed | tf_op | source)
XLA Modules:
  0.0 180.3 jit_solution(12147934878845846653)
XLA Ops:
  0.6 176.7 %shard_map.95 = (bf16[2,32,2048]{2,1,0:T(8,128)(2,1)}, bf16[6,2,32]{2,1,0:T(2,128)(2,1)}) custom-call(bf16[2,32,2048]{2,1,0:T(8,128)(2,1)} %og_ref.1, bf16[32,2048]{1,0:T(8,128)(2,1)} %cg_ref.1, bf16[2,32,2048]{2,1,0:T(8,128)(2,1)} %bitcast.21, s32[6,2,32]{2,1,0:T(2,128)} %bitcast.23, bf16[6,2,32]{2,1,0:T(2,128)(2,1)} %bitcast.24, ...), custom_call_target="tpu_custom_call" | custom-call | tf_op jit(solution)/shard_map/pallas_call | solution.py:505
  177.3 1.7 copy.12
  179.0 1.3 copy.13

commit v3 on v2

--- a/solution.py
+++ b/solution.py
@@ -312,10 +312,10 @@
         drain(came[c].at[m, pl.ds(0, NG - 1)], r_rs.at[m, c])
         rows = came[c][m].reshape(ROWS, WIDE[c])
         value = jnp.dot(cmat[m], rows[:, :W], preferred_element_type=F32)
-        sums[c][:, :, :W] = value.reshape(NZ, TOK, W)
+        sums[c][m, :, :, :W] = value.reshape(NZ, TOK, W)
         if c == 1:
             extra = jnp.dot(mmat[m], rows[:, W:], preferred_element_type=F32)
-            sums[c][:, :, W:] = extra.reshape(NZ, TOK, EXTRA)
+            sums[c][m, :, :, W:] = extra.reshape(NZ, TOK, EXTRA)
 
     def scatter(m, c):
         nr, nl = STEPS[c]
@@ -337,7 +337,7 @@
                 if s < count:
                     slot = s if direction == 0 else nr + s
                     dest = lax.rem(z + nr - s, NZ) if direction == 0 else lax.rem(z - nl + s + NZ, NZ)
-                    value = sums[c][dest]
+                    value = sums[c][m, dest]
                     if s >= 1:
                         value = value + rs_recv[m, c, slot - 1, :, :width].astype(F32)
                     rs_send[m, c, slot, :, :width] = value.astype(BF16)
@@ -354,7 +354,7 @@
         for c in range(HALVES):
             nr, nl = STEPS[c]
             width = WIDE[c]
-            total = sums[c][z]
+            total = sums[c][m, z]
             total += rs_recv[m, c, nr - 1, :, :width].astype(F32)
             total += rs_recv[m, c, nr + nl - 1, :, :width].astype(F32)
             cols = slice(c * W, (c + 1) * W)
@@ -468,9 +468,27 @@
 
     @pl.when(first)
     def _():
-        collect(0)
-
-    collect(1)
+        for c in both:
+            combine(0, c)
+        hops = [[scatter(m, c) for c in both] for m in range(2)]
+        for s in range(3):
+            for hop in hops[0]:
+                hop[0](s)
+        for c in both:
+            combine(1, c)
+        for s in range(5):
+            for hop in hops[1]:
+                hop[0](s)
+            if s < 2:
+                for hop in hops[0]:
+                    hop[0](s + 3)
+            if s == 2:
+                finish(0)
+        finish(1)
+
+    @pl.when(last)
+    def _():
+        collect(1)
 
     for item in items + second_x + [scatter(m, c) for m in range(2) for c in both]:
         item[2]()
@@ -536,8 +554,8 @@
             pltpu.VMEM((2, ROWS, ALL), BF16),
             pltpu.VMEM((2, ALL, ROWS), BF16),
             pltpu.VMEM((2, ALL, ROWS), BF16),
-            pltpu.VMEM((NZ, TOK, WIDE[0]), F32),
-            pltpu.VMEM((NZ, TOK, WIDE[1]), F32),
+            pltpu.VMEM((2, NZ, TOK, WIDE[0]), F32),
+            pltpu.VMEM((2, NZ, TOK, WIDE[1]), F32),
             pltpu.VMEM((*both, NZ - 1, TOK, WIDE[1]), BF16),
             pltpu.VMEM((*both, NZ - 1, TOK, WIDE[1]), BF16),
             dma((3,)),

time: 180 us -> 176 us (0.978)
  Pallas kernels: 177 us -> 172 us
    pallas_call x1, Pallas kernels: 177 us -> 172 us  [local(): pl.pallas_call(kernel, out_shape=(jax.ShapeDtypeStruct((2, TOK, D), BF16)...]
where the time goes in v3:
time: 176 us; the launch traced here: 175 us
  Pallas kernels  172 us (98%)
  local copies, waits for them, and re-layouts  2.92 us (2%)
    pallas_call x1, Pallas kernels, local(): pl.pallas_call(kernel, out_shape=(jax.ShapeDtypeStruct((2, TOK, D), BF16)...  172 us

profile of v3, /device:TPU:8, one launch (start us, length us, event | category | flops | bytes accessed | tf_op | source)
XLA Modules:
  0.0 175.4 jit_solution(8323792756592567828)
XLA Ops:
  0.6 171.8 %shard_map.95 = (bf16[2,32,2048]{2,1,0:T(8,128)(2,1)}, bf16[6,2,32]{2,1,0:T(2,128)(2,1)}) custom-call(bf16[2,32,2048]{2,1,0:T(8,128)(2,1)} %og_ref.1, bf16[32,2048]{1,0:T(8,128)(2,1)} %cg_ref.1, bf16[2,32,2048]{2,1,0:T(8,128)(2,1)} %bitcast.21, s32[6,2,32]{2,1,0:T(2,128)} %bitcast.23, bf16[6,2,32]{2,1,0:T(2,128)(2,1)} %bitcast.24, ...), custom_call_target="tpu_custom_call" | custom-call | tf_op jit(solution)/shard_map/pallas_call | solution.py:523
  172.4 1.7 copy.12
  174.1 1.3 copy.13
